TPU v7x, 32 devices: a whole 2x2x4 slice. The times are simulated.
32 devices in a mesh: dp: 4 (over y, x), tm: 4 (over z), rows: 2 (over core).
Axes of the slice: x: 2, y: 2, z: 4, core: 2. Of those that a mesh axis runs over, the one named last changes fastest.
Arguments:
- latents: bfloat16 [4, 8, 8, 32, 384], P('dp', 'tm', 'rows'), may hold values from -6 to 6
- hidden: bfloat16 [4, 8, 8, 32, 384], P('dp', 'tm', 'rows'), may hold values from -8 to 8
- cotangent: bfloat16 [4, 8, 8, 32, 384], P('dp', 'tm', 'rows'), may hold values from -6 to 6
- conv_one: bfloat16 [3, 3, 3, 384, 384], replicated, may hold values from -0.0625 to 0.0625
- conv_two: bfloat16 [3, 3, 3, 384, 384], replicated, may hold values from -0.0625 to 0.0625
- lengths: int32 [4], P('dp'), may hold values from 3 to 8, as said below
Outputs:
- latent_grad: float32 [4, 8, 8, 32, 384], P('dp', None, None, ('tm', 'rows'))
Inputs may be any that keep to these rules, and one draw needn't show every extreme that they name: `lengths`: at least one clip has all 8 frames valid.
All inputs are finite; a program needn't handle non-finite values.
Results may differ from a plain program's by a relative error of at most 0.00092.
Values may be sent and summed in bfloat16 or wider, within the bound.
No kernel may reach another device: no remote copies, remote signals or barrier semaphores. Data moves between devices by JAX's collectives and lax.ppermute only.
A program may use at most 64 MiB of HBM per device.

v0:
```python
import jax
import jax.numpy as jnp
from jax import lax
from jax.sharding import PartitionSpec as P


def with_halo(block, sides, width):
    for axis, dim in sides:
        count = lax.axis_size(axis)
        forward = [(i, i + 1) for i in range(count - 1)]
        backward = [(target, source) for source, target in forward]
        low = lax.ppermute(
            lax.slice_in_dim(block, block.shape[dim] - width, None, axis=dim), axis, forward
        )
        high = lax.ppermute(lax.slice_in_dim(block, 0, width, axis=dim), axis, backward)
        block = jnp.concatenate([low, block, high], axis=dim)
    return block


def shifted(value, axis, by):
    devices = lax.axis_size(axis)
    pairs = [(i, i + by) for i in range(devices) if 0 <= i + by < devices]
    return lax.ppermute(value, axis, pairs)


def silu_slope(values):
    sigmoid_of = jax.nn.sigmoid(values)
    return sigmoid_of * (1.0 + values * (1.0 - sigmoid_of))


def extended(row_band, next_frames):
    joined = jnp.concatenate([row_band, next_frames], axis=0)
    return jnp.pad(joined, ((0, 0), (0, 0), (1, 1), (0, 0)))


def transposed_conv(padded, kernel, frame_count, row_count, col_count):
    summed = jnp.zeros((frame_count, row_count, col_count, kernel.shape[4]), jnp.float32)
    for time_tap in range(3):
        for row_tap in range(3):
            slab_rows = padded[time_tap : time_tap + frame_count, row_tap : row_tap + row_count]
            stacked = jnp.stack(
                [slab_rows[:, :, col_tap : col_tap + col_count] for col_tap in range(3)], axis=3
            )
            kernel_slice = kernel[2 - time_tap, 2 - row_tap, ::-1]
            summed = summed + jnp.einsum(
                "frwkc,kdc->frwd", stacked, kernel_slice, preferred_element_type=jnp.float32
            )
    return summed


def on_device(latents, hidden, cotangent, conv_one, conv_two, lengths):
    frame_dev = latents.shape[1]
    row_dev = latents.shape[2]
    col_count = latents.shape[3]
    channels = latents.shape[4]
    first_frame = lax.axis_index("tm") * frame_dev
    frames = first_frame + jnp.arange(frame_dev, dtype=jnp.int32)
    live_frames = frames < lengths[0]
    masked = jnp.where(live_frames[:, None, None, None], cotangent[0], jnp.zeros_like(cotangent[0]))
    cot_band = with_halo(masked, (("rows", 1),), 1)
    cot_next = shifted(cot_band, "tm", -1)
    grad_act = transposed_conv(
        extended(cot_band, cot_next), conv_two, frame_dev, row_dev, col_count
    )
    grad_hidden = (grad_act * silu_slope(hidden[0].astype(jnp.float32))).astype(jnp.bfloat16)
    hidden_band = with_halo(grad_hidden, (("rows", 1),), 1)
    hidden_next = shifted(hidden_band, "tm", -1)
    grad_input = transposed_conv(
        extended(hidden_band, hidden_next), conv_one, frame_dev, row_dev, col_count
    )
    result = masked.astype(jnp.float32) + grad_input * silu_slope(latents[0].astype(jnp.float32))
    result = result[None]
    time_devs = lax.axis_size("tm")
    row_devs = lax.axis_size("rows")
    arrived = lax.all_to_all(
        result[:, None], ("tm", "rows"), split_axis=4, concat_axis=1, tiled=True
    )
    col_dev = arrived.shape[4]
    arranged = arrived.reshape(1, time_devs, row_devs, frame_dev, row_dev, col_dev, channels)
    arranged = arranged.transpose(0, 1, 3, 2, 4, 5, 6)
    return arranged.reshape(1, time_devs * frame_dev, row_devs * row_dev, col_dev, channels)


def solution(mesh):
    in_specs = (
        P("dp", "tm", "rows", None, None),
        P("dp", "tm", "rows", None, None),
        P("dp", "tm", "rows", None, None),
        P(),
        P(),
        P("dp"),
    )
    out_specs = P("dp", None, None, ("tm", "rows"), None)
    return jax.shard_map(
        on_device, mesh=mesh, in_specs=in_specs, out_specs=out_specs, check_vma=False
    )
```

profile of v0, /device:TPU:0, one launch (start us, length us, event | category | flops | bytes accessed | tf_op | source)
XLA Modules:
  0.0 96.8 jit_solution(17803353701645760821)
XLA Ops:
  1.7 2.4 %collective-permute-start = (bf16[2,1,32,384]{3,2,1,0:T(8,128)(2,1)S(1)}, bf16[2,1,32,384]{3,2,1,0:T(8,128)(2,1)S(1)}, u32[]{:S(2)}, u32[]{:S(2)}) collective-permute-start(bf16[2,1,32,384]{3,2,1,0:T(8,128)(2,1)S(1)} %get-tuple-element.77), channel_id=1, source_target_pairs={{0,1},{2,3},{4,5},{6,7},{8,9},{10,11},{12,13},{14,15},{16,17},{18,... | collective-permute-start | bytes 147464 | tf_op jit(solution)/shard_map/ppermute | solution.py:12
  4.1 1.3 %collective-permute-start.1 = (bf16[2,1,32,384]{3,2,1,0:T(8,128)(2,1)S(1)}, bf16[2,1,32,384]{3,2,1,0:T(8,128)(2,1)S(1)}, u32[]{:S(2)}, u32[]{:S(2)}) collective-permute-start(bf16[2,1,32,384]{3,2,1,0:T(8,128)(2,1)S(1)} %get-tuple-element.78), channel_id=1, source_target_pairs={{1,0},{3,2},{5,4},{7,6},{9,8},{11,10},{13,12},{15,14},{17,16},{19,... | collective-permute-start | bytes 147464 | tf_op jit(solution)/shard_map/ppermute | solution.py:15
  5.4 5.3 %fusion.122 = (bf16[1,1,3,384,384]{4,3,2,1,0:T(8,128)(2,1)}, bf16[1,1,3,384,384]{4,3,2,1,0:T(8,128)(2,1)S(1)}, bf16[1,1,3,384,384]{4,3,2,1,0:T(8,128)(2,1)S(1)},...) fusion(bf16[3,3,3,384,384]{4,3,2,1,0:T(8,128)(2,1)} %param.10), kind=kLoop, calls=%fused_computation.211 | loop fusion | bytes 15925248 | tf_op jit(solution)/shard_map/slice | solution.py:44
  10.7 2.2 %rev.55 = bf16[1,1,3,384,384]{4,3,2,1,0:T(8,128)(2,1)} reverse(bf16[1,1,3,384,384]{4,3,2,1,0:T(8,128)(2,1)} %get-tuple-element.14), dimensions={2} | reverse | bytes 1769472 | tf_op jit(solution)/shard_map/rev | solution.py:44
  12.9 2.2 %rev.56 = bf16[1,1,3,384,384]{4,3,2,1,0:T(8,128)(2,1)} reverse(bf16[1,1,3,384,384]{4,3,2,1,0:T(8,128)(2,1)} %get-tuple-element.19), dimensions={2} | reverse | bytes 1769472 | tf_op jit(solution)/shard_map/rev | solution.py:44
  15.1 2.2 %rev.57 = bf16[1,1,3,384,384]{4,3,2,1,0:T(8,128)(2,1)} reverse(bf16[1,1,3,384,384]{4,3,2,1,0:T(8,128)(2,1)} %get-tuple-element.18), dimensions={2} | reverse | bytes 1769472 | tf_op jit(solution)/shard_map/rev | solution.py:44
  17.3 2.2 %rev.58 = bf16[1,1,3,384,384]{4,3,2,1,0:T(8,128)(2,1)} reverse(bf16[1,1,3,384,384]{4,3,2,1,0:T(8,128)(2,1)} %get-tuple-element.17), dimensions={2} | reverse | bytes 1769472 | tf_op jit(solution)/shard_map/rev | solution.py:44
  20.7 1.3 %rev.62 = bf16[1,1,3,384,384]{4,3,2,1,0:T(8,128)(2,1)S(1)} reverse(bf16[1,1,3,384,384]{4,3,2,1,0:T(8,128)(2,1)} %get-tuple-element.21), dimensions={2} | reverse | bytes 1769472 | tf_op jit(solution)/shard_map/rev | solution.py:44
  22.0 2.2 %rev.54 = bf16[1,1,3,384,384]{4,3,2,1,0:T(8,128)(2,1)} reverse(bf16[1,1,3,384,384]{4,3,2,1,0:T(8,128)(2,1)} %get-tuple-element.20), dimensions={2} | reverse | bytes 1769472 | tf_op jit(solution)/shard_map/rev | solution.py:44
  24.2 1.4 %collective-permute-start.2 = (bf16[2,6,32,384]{3,2,1,0:T(8,128)(2,1)S(1)}, bf16[2,6,32,384]{3,2,1,0:T(8,128)(2,1)S(1)}, u32[]{:S(2)}, u32[]{:S(2)}) collective-permute-start(bf16[2,6,32,384]{3,2,1,0:T(8,128)(2,1)S(1)} %pad_maximum_fusion.19), channel_id=1, source_target_pairs={{2,0},{4,2},{6,4},{3,1},{5,3},{7,5},{10,8},{12,10},{14,12},{11,9},... | collective-permute-start | bytes 884744 | tf_op jit(solution)/shard_map/ppermute | solution.py:23
  25.8 10.3 %collective-permute-done.2 = bf16[2,6,32,384]{3,2,1,0:T(8,128)(2,1)S(1)} collective-permute-done((bf16[2,6,32,384]{3,2,1,0:T(8,128)(2,1)S(1)}, bf16[2,6,32,384]{3,2,1,0:T(8,128)(2,1)S(1)}, u32[]{:S(2)}, u32[]{:S(2)}) %collective-permute-start.2) | collective-permute-done | bytes 294944 | tf_op jit(solution)/shard_map/ppermute | solution.py:23
  42.4 2.2 %collective-permute-start.3 = (bf16[2,1,32,384]{3,2,1,0:T(8,128)(2,1)S(1)}, bf16[2,1,32,384]{3,2,1,0:T(8,128)(2,1)S(1)}, u32[]{:S(2)}, u32[]{:S(2)}) collective-permute-start(bf16[2,1,32,384]{3,2,1,0:T(8,128)(2,1)S(1)} %get-tuple-element.73), channel_id=1, source_target_pairs={{0,1},{2,3},{4,5},{6,7},{8,9},{10,11},{12,13},{14,15},{16,17},{18,... | collective-permute-start | bytes 147464 | tf_op jit(solution)/shard_map/ppermute | solution.py:12
  44.6 1.3 %collective-permute-start.4 = (bf16[2,1,32,384]{3,2,1,0:T(8,128)(2,1)S(1)}, bf16[2,1,32,384]{3,2,1,0:T(8,128)(2,1)S(1)}, u32[]{:S(2)}, u32[]{:S(2)}) collective-permute-start(bf16[2,1,32,384]{3,2,1,0:T(8,128)(2,1)S(1)} %get-tuple-element.74), channel_id=1, source_target_pairs={{1,0},{3,2},{5,4},{7,6},{9,8},{11,10},{13,12},{15,14},{17,16},{19,... | collective-permute-start | bytes 147464 | tf_op jit(solution)/shard_map/ppermute | solution.py:15
  45.9 1.8 %collective-permute-done.4 = bf16[2,1,32,384]{3,2,1,0:T(8,128)(2,1)S(1)} collective-permute-done((bf16[2,1,32,384]{3,2,1,0:T(8,128)(2,1)S(1)}, bf16[2,1,32,384]{3,2,1,0:T(8,128)(2,1)S(1)}, u32[]{:S(2)}, u32[]{:S(2)}) %collective-permute-start.4) | collective-permute-done | bytes 49184 | tf_op jit(solution)/shard_map/ppermute | solution.py:15
  48.5 1.5 %collective-permute-start.5 = (bf16[2,6,32,384]{3,2,1,0:T(8,128)(2,1)}, bf16[2,6,32,384]{3,2,1,0:T(8,128)(2,1)}, u32[]{:S(2)}, u32[]{:S(2)}) collective-permute-start(bf16[2,6,32,384]{3,2,1,0:T(8,128)(2,1)} %pad_maximum_fusion.20), channel_id=1, source_target_pairs={{2,0},{4,2},{6,4},{3,1},{5,3},{7,5},{10,8},{12,10},{14,12},{11,9},... | collective-permute-start | bytes 884744 | tf_op jit(solution)/shard_map/ppermute | solution.py:23
  50.0 2.7 %fusion.121 = (bf16[1,1,3,384,384]{4,3,2,1,0:T(8,128)(2,1)}, bf16[1,1,3,384,384]{4,3,2,1,0:T(8,128)(2,1)S(1)}, bf16[1,1,3,384,384]{4,3,2,1,0:T(8,128)(2,1)S(1)},...) fusion(bf16[3,3,3,384,384]{4,3,2,1,0:T(8,128)(2,1)S(1)} %bitcas, ...), kind=kLoop, calls=%fused_computation.210 | loop fusion | bytes 15925248 | tf_op jit(solution)/shard_map/slice | solution.py:44
  52.7 2.2 %rev.63 = bf16[1,1,3,384,384]{4,3,2,1,0:T(8,128)(2,1)} reverse(bf16[1,1,3,384,384]{4,3,2,1,0:T(8,128)(2,1)} %get-tuple-element.5), dimensions={2} | reverse | bytes 1769472 | tf_op jit(solution)/shard_map/rev | solution.py:44
  54.9 2.2 %rev.64 = bf16[1,1,3,384,384]{4,3,2,1,0:T(8,128)(2,1)} reverse(bf16[1,1,3,384,384]{4,3,2,1,0:T(8,128)(2,1)} %get-tuple-element.11), dimensions={2} | reverse | bytes 1769472 | tf_op jit(solution)/shard_map/rev | solution.py:44
  57.1 2.2 %rev.65 = bf16[1,1,3,384,384]{4,3,2,1,0:T(8,128)(2,1)} reverse(bf16[1,1,3,384,384]{4,3,2,1,0:T(8,128)(2,1)} %get-tuple-element.10), dimensions={2} | reverse | bytes 1769472 | tf_op jit(solution)/shard_map/rev | solution.py:44
  59.3 2.2 %rev.66 = bf16[1,1,3,384,384]{4,3,2,1,0:T(8,128)(2,1)} reverse(bf16[1,1,3,384,384]{4,3,2,1,0:T(8,128)(2,1)} %get-tuple-element.9), dimensions={2} | reverse | bytes 1769472 | tf_op jit(solution)/shard_map/rev | solution.py:44
  61.4 2.2 %rev.67 = bf16[1,1,3,384,384]{4,3,2,1,0:T(8,128)(2,1)} reverse(bf16[1,1,3,384,384]{4,3,2,1,0:T(8,128)(2,1)} %get-tuple-element.8), dimensions={2} | reverse | bytes 1769472 | tf_op jit(solution)/shard_map/rev | solution.py:44
  69.0 1.7 %fusion.26 = f32[2,4,32,384,1]{3,2,0,1,4:T(8,128)S(1)} fusion(bf16[1,1,3,384,384]{4,3,2,1,0:T(8,128)(2,1)} %rev.63, bf16[2,4,32,1,384]{4,2,1,0,3:T(8,128)(2,1)S(1)} %get-tuple-element.24, bf16[2,4,32,1,384]{4,2,1,0,3:T(8,128)(2,1)S(1)} %get-tuple-element.71, bf16[2,4,32,1,384]{4,2,1,0,3:T(8,128)(2,1)S(1)} %get-tuple-element.23), kind=kOutput, calls=%fused_computation.27 | convolution fusion | flops 227082240 | bytes 1867776 | tf_op jit(solution)/shard_map/frwkc,kdc->frwd/dot_general | solution.py:45
  73.3 1.2 %slice_bitcast_fusion.2 = (bf16[2,4,32,1,384]{4,2,1,0,3:T(8,128)(2,1)S(1)}, bf16[2,4,32,1,384]{4,2,1,0,3:T(8,128)(2,1)S(1)}, bf16[2,4,32,1,384]{4,2,1,0,3:T(8,128)(2,1)S(1)}) fusion(bf16[2,6,32,384]{3,2,1,0:T(8,128)(2,1)} %collective-permute-done.5), kind=kLoop, calls=%fused_computation.188 | loop fusion | bytes 1179648 | tf_op jit(solution)/shard_map/stack | solution.py:41
  76.7 19.3 %all_to_all.15 = f32[1,1,2,4,32,384]{5,3,2,1,0,4:T(4,128)S(1)} all-to-all(f32[1,1,2,4,32,384]{5,3,2,1,0,4:T(4,128)S(1)} %copy.46), channel_id=1, replica_groups=mesh['dp'=4,'tm'=4,'rows'=2] {'tm','rows'}, dimensions={4} | all-to-all | bytes 786432 | tf_op jit(solution)/shard_map/all_to_all | solution.py:75
  (96 shorter events, 20.0 us)
Async XLA Ops:
  1.7 22.4 %collective-permute-start = (bf16[2,1,32,384]{3,2,1,0:T(8,128)(2,1)S(1)}, bf16[2,1,32,384]{3,2,1,0:T(8,128)(2,1)S(1)}, u32[]{:S(2)}, u32[]{:S(2)}) collective-permute-start(bf16[2,1,32,384]{3,2,1,0:T(8,128)(2,1)S(1)} %get-tuple-element.77), channel_id=1, source_target_pairs={{0,1},{2,3},{4,5},{6,7},{8,9},{10,11},{12,13},{14,15},{16,17},{18,... | collective-permute-start | bytes 147464 | tf_op jit(solution)/shard_map/ppermute | solution.py:12
  4.1 20.0 %collective-permute-start.1 = (bf16[2,1,32,384]{3,2,1,0:T(8,128)(2,1)S(1)}, bf16[2,1,32,384]{3,2,1,0:T(8,128)(2,1)S(1)}, u32[]{:S(2)}, u32[]{:S(2)}) collective-permute-start(bf16[2,1,32,384]{3,2,1,0:T(8,128)(2,1)S(1)} %get-tuple-element.78), channel_id=1, source_target_pairs={{1,0},{3,2},{5,4},{7,6},{9,8},{11,10},{13,12},{15,14},{17,16},{19,... | collective-permute-start | bytes 147464 | tf_op jit(solution)/shard_map/ppermute | solution.py:15
  10.7 14.9 %copy-start.7 = (bf16[1,2,4,32,384]{4,3,2,1,0:T(8,128)(2,1)S(1)}, bf16[1,2,4,32,384]{4,3,2,1,0:T(8,128)(2,1)}, u32[]{:S(2)}) copy-start(bf16[1,2,4,32,384]{4,3,2,1,0:T(8,128)(2,1)} %param.8) | copy-start | bytes 589828
  24.2 12.9 %copy-start.4 = (bf16[1,1,3,384,384]{4,3,2,1,0:T(8,128)(2,1)S(1)}, bf16[1,1,3,384,384]{4,3,2,1,0:T(8,128)(2,1)}, u32[]{:S(2)}) copy-start(bf16[1,1,3,384,384]{4,3,2,1,0:T(8,128)(2,1)} %rev.55) | copy-start | bytes 2654212
  24.2 13.4 %copy-start.3 = (bf16[1,1,3,384,384]{4,3,2,1,0:T(8,128)(2,1)S(1)}, bf16[1,1,3,384,384]{4,3,2,1,0:T(8,128)(2,1)}, u32[]{:S(2)}) copy-start(bf16[1,1,3,384,384]{4,3,2,1,0:T(8,128)(2,1)} %rev.56) | copy-start | bytes 2654212
  24.2 11.8 %collective-permute-start.2 = (bf16[2,6,32,384]{3,2,1,0:T(8,128)(2,1)S(1)}, bf16[2,6,32,384]{3,2,1,0:T(8,128)(2,1)S(1)}, u32[]{:S(2)}, u32[]{:S(2)}) collective-permute-start(bf16[2,6,32,384]{3,2,1,0:T(8,128)(2,1)S(1)} %pad_maximum_fusion.19), channel_id=1, source_target_pairs={{2,0},{4,2},{6,4},{3,1},{5,3},{7,5},{10,8},{12,10},{14,12},{11,9},... | collective-permute-start | bytes 884744 | tf_op jit(solution)/shard_map/ppermute | solution.py:23
  25.8 12.5 %copy-start.2 = (bf16[1,1,3,384,384]{4,3,2,1,0:T(8,128)(2,1)S(1)}, bf16[1,1,3,384,384]{4,3,2,1,0:T(8,128)(2,1)}, u32[]{:S(2)}) copy-start(bf16[1,1,3,384,384]{4,3,2,1,0:T(8,128)(2,1)} %rev.57) | copy-start | bytes 2654212
  38.8 3.0 %copy-start.9 = (bf16[1,1,3,384,384]{4,3,2,1,0:T(8,128)(2,1)S(1)}, bf16[1,1,3,384,384]{4,3,2,1,0:T(8,128)(2,1)}, u32[]{:S(2)}) copy-start(bf16[1,1,3,384,384]{4,3,2,1,0:T(8,128)(2,1)} %rev.54) | copy-start | bytes 2654212
  38.8 3.0 %copy-start.19 = (bf16[1,2,4,32,384]{4,3,2,1,0:T(8,128)(2,1)S(1)}, bf16[1,2,4,32,384]{4,3,2,1,0:T(8,128)(2,1)}, u32[]{:S(2)}) copy-start(bf16[1,2,4,32,384]{4,3,2,1,0:T(8,128)(2,1)} %param.7) | copy-start | bytes 589828
  40.0 9.9 %slice-start = ((s8[7962624]{0:T(1024)(128)(4,1)}), s8[4194304]{0:T(1024)(128)(4,1)S(1)}, s32[]{:S(2)}) async-start(s8[7962624]{0:T(1024)(128)(4,1)} %bitcast.332), calls=%async_computation.1 | async-start | bytes 8388608
  41.2 8.8 %slice-start.1 = ((s8[7962624]{0:T(1024)(128)(4,1)}), s8[3768320]{0:T(1024)(128)(4,1)S(1)}, s32[]{:S(2)}) async-start(s8[7962624]{0:T(1024)(128)(4,1)} %bitcast.332), calls=%async_computation.2 | async-start | bytes 7536640
  42.4 6.1 %copy-start.5 = (bf16[2,4,32,384]{3,2,1,0:T(8,128)(2,1)}, bf16[2,4,32,384]{3,2,1,0:T(8,128)(2,1)S(1)}, u32[]{:S(2)}) copy-start(bf16[2,4,32,384]{3,2,1,0:T(8,128)(2,1)S(1)} %fusion.9) | copy-start | bytes 589828
  42.4 3.5 %collective-permute-start.3 = (bf16[2,1,32,384]{3,2,1,0:T(8,128)(2,1)S(1)}, bf16[2,1,32,384]{3,2,1,0:T(8,128)(2,1)S(1)}, u32[]{:S(2)}, u32[]{:S(2)}) collective-permute-start(bf16[2,1,32,384]{3,2,1,0:T(8,128)(2,1)S(1)} %get-tuple-element.73), channel_id=1, source_target_pairs={{0,1},{2,3},{4,5},{6,7},{8,9},{10,11},{12,13},{14,15},{16,17},{18,... | collective-permute-start | bytes 147464 | tf_op jit(solution)/shard_map/ppermute | solution.py:12
  44.6 3.1 %collective-permute-start.4 = (bf16[2,1,32,384]{3,2,1,0:T(8,128)(2,1)S(1)}, bf16[2,1,32,384]{3,2,1,0:T(8,128)(2,1)S(1)}, u32[]{:S(2)}, u32[]{:S(2)}) collective-permute-start(bf16[2,1,32,384]{3,2,1,0:T(8,128)(2,1)S(1)} %get-tuple-element.74), channel_id=1, source_target_pairs={{1,0},{3,2},{5,4},{7,6},{9,8},{11,10},{13,12},{15,14},{17,16},{19,... | collective-permute-start | bytes 147464 | tf_op jit(solution)/shard_map/ppermute | solution.py:15
  48.5 18.6 %collective-permute-start.5 = (bf16[2,6,32,384]{3,2,1,0:T(8,128)(2,1)}, bf16[2,6,32,384]{3,2,1,0:T(8,128)(2,1)}, u32[]{:S(2)}, u32[]{:S(2)}) collective-permute-start(bf16[2,6,32,384]{3,2,1,0:T(8,128)(2,1)} %pad_maximum_fusion.20), channel_id=1, source_target_pairs={{2,0},{4,2},{6,4},{3,1},{5,3},{7,5},{10,8},{12,10},{14,12},{11,9},... | collective-permute-start | bytes 884744 | tf_op jit(solution)/shard_map/ppermute | solution.py:23
  64.7 6.0 %copy-start.6 = (bf16[2,4,32,384]{3,2,1,0:T(8,128)(2,1)S(1)}, bf16[2,4,32,384]{3,2,1,0:T(8,128)(2,1)}, u32[]{:S(2)}) copy-start(bf16[2,4,32,384]{3,2,1,0:T(8,128)(2,1)} %copy-done.5) | copy-start | bytes 589828
  65.9 4.8 %copy-start.15 = (bf16[1,1,3,384,384]{4,3,2,1,0:T(8,128)(2,1)S(1)}, bf16[1,1,3,384,384]{4,3,2,1,0:T(8,128)(2,1)}, u32[]{:S(2)}) copy-start(bf16[1,1,3,384,384]{4,3,2,1,0:T(8,128)(2,1)} %rev.64) | copy-start | bytes 2654212
  65.9 5.4 %copy-start.14 = (bf16[1,1,3,384,384]{4,3,2,1,0:T(8,128)(2,1)S(1)}, bf16[1,1,3,384,384]{4,3,2,1,0:T(8,128)(2,1)}, u32[]{:S(2)}) copy-start(bf16[1,1,3,384,384]{4,3,2,1,0:T(8,128)(2,1)} %rev.65) | copy-start | bytes 2654212
  65.9 5.8 %copy-start.13 = (bf16[1,1,3,384,384]{4,3,2,1,0:T(8,128)(2,1)S(1)}, bf16[1,1,3,384,384]{4,3,2,1,0:T(8,128)(2,1)}, u32[]{:S(2)}) copy-start(bf16[1,1,3,384,384]{4,3,2,1,0:T(8,128)(2,1)} %rev.66) | copy-start | bytes 2654212
  68.2 4.0 %copy-start.12 = (bf16[1,1,3,384,384]{4,3,2,1,0:T(8,128)(2,1)S(1)}, bf16[1,1,3,384,384]{4,3,2,1,0:T(8,128)(2,1)}, u32[]{:S(2)}) copy-start(bf16[1,1,3,384,384]{4,3,2,1,0:T(8,128)(2,1)} %rev.67) | copy-start | bytes 2654212
  68.9 3.9 %copy-start.11 = (bf16[1,1,3,384,384]{4,3,2,1,0:T(8,128)(2,1)S(1)}, bf16[1,1,3,384,384]{4,3,2,1,0:T(8,128)(2,1)}, u32[]{:S(2)}) copy-start(bf16[1,1,3,384,384]{4,3,2,1,0:T(8,128)(2,1)} %rev.68) | copy-start | bytes 2654212
  70.7 3.7 %copy-start.10 = (bf16[1,1,3,384,384]{4,3,2,1,0:T(8,128)(2,1)S(1)}, bf16[1,1,3,384,384]{4,3,2,1,0:T(8,128)(2,1)}, u32[]{:S(2)}) copy-start(bf16[1,1,3,384,384]{4,3,2,1,0:T(8,128)(2,1)} %rev.69) | copy-start | bytes 2654212
  72.2 3.7 %copy-start.8 = (bf16[1,2,4,32,384]{4,3,2,1,0:T(8,128)(2,1)S(1)}, bf16[1,2,4,32,384]{4,3,2,1,0:T(8,128)(2,1)}, u32[]{:S(2)}) copy-start(bf16[1,2,4,32,384]{4,3,2,1,0:T(8,128)(2,1)} %param.8) | copy-start | bytes 589828
  72.3 3.7 %copy-start.18 = (bf16[1,2,4,32,384]{4,3,2,1,0:T(8,128)(2,1)S(1)}, bf16[1,2,4,32,384]{4,3,2,1,0:T(8,128)(2,1)}, u32[]{:S(2)}) copy-start(bf16[1,2,4,32,384]{4,3,2,1,0:T(8,128)(2,1)} %param.6) | copy-start | bytes 589828
  (4 other events, 8.6 us)
where the time goes:
time: 97.7 us; the launch traced here: 96.8 us
  local copies, waits for them, and re-layouts  38.4 us (39%)
  blocking collectives  19.3 us (20%)
  waiting for transfers between devices  12.1 us (12%)
  matrix products  10.2 us (10%)
  starting transfers between devices  10 us (10%)
  other arithmetic  5.43 us (6%)
  between operations  1.33 us (1%)
    rev x18, local copies, waits for them, and re-layouts, transposed_conv(): kernel_slice = kernel[2 - time_tap, 2 - row_tap, ::-1]  26.5 us
    all_to_all x1, blocking collectives, on_device(): lax.all_to_all(result[:, None], ('tm', 'rows'), split_axis=4, concat_axis...  19.3 us
    ppermute x2, waiting for transfers between devices, shifted(): return lax.ppermute(value, axis, pairs)  10.3 us
    dot_general x18, matrix products, transposed_conv(): jnp.einsum('frwkc,kdc->frwd', stacked, kernel_slice, preferred_element_ty...  10.2 us
    slice x2, local copies, waits for them, and re-layouts, transposed_conv(): kernel_slice = kernel[2 - time_tap, 2 - row_tap, ::-1]  8.04 us
    ppermute x2, starting transfers between devices, with_halo(): lax.ppermute(lax.slice_in_dim(block, block.shape[dim] - width, None, axis...  4.57 us
    ppermute x2, starting transfers between devices, shifted(): return lax.ppermute(value, axis, pairs)  2.89 us
    another operation x6, local copies, waits for them, and re-layouts, transposed_conv(): jnp.stack([slab_rows[:, :, col_tap:col_tap + col_count] for col_tap in ra...  2.65 us
  transfers between devices with their start and end apart: 6, of which 2 were waited for; matrix products, arithmetic and copies ran while one was open for 37% of the time, Pallas kernels for 0%

commit v1 on v0

--- a/solution.py
+++ b/solution.py
@@ -72,9 +72,20 @@
     result = result[None]
     time_devs = lax.axis_size("tm")
     row_devs = lax.axis_size("rows")
-    arrived = lax.all_to_all(
-        result[:, None], ("tm", "rows"), split_axis=4, concat_axis=1, tiled=True
-    )
+    x = result[:, None]
+    ways, here = (lax.axis_size(("tm", "rows")), lax.axis_index(("tm", "rows")))
+    width_2 = x.shape[4] // ways
+    dims = list(x.shape)
+    dims[4] = width_2
+    height = dims[1]
+    dims[1] = height * ways
+    full = jnp.zeros(dims, x.dtype)
+    for mask in range(ways):
+        part = lax.dynamic_slice_in_dim(x, (here ^ mask) * width_2, width_2, axis=4)
+        if mask:
+            part = lax.ppermute(part, ("tm", "rows"), [(d, d ^ mask) for d in range(ways)])
+        full = lax.dynamic_update_slice_in_dim(full, part, (here ^ mask) * height, axis=1)
+    arrived = full
     col_dev = arrived.shape[4]
     arranged = arrived.reshape(1, time_devs, row_devs, frame_dev, row_dev, col_dev, channels)
     arranged = arranged.transpose(0, 1, 3, 2, 4, 5, 6)

time: 97.7 us -> 94.4 us (0.966)
  blocking collectives: 19.3 us -> 0 us
  starting transfers between devices: 10 us -> 20.5 us
  waiting for transfers between devices: 12.1 us -> 17.5 us
    all_to_all x1 -> x0, blocking collectives: 19.3 us -> none  [on_device(): lax.all_to_all(result[:, None], ('tm', 'rows'), split_axis=4, concat_axis...]
    ppermute x0 -> x7, starting transfers between devices: none -> 10.5 us  [on_device(): lax.ppermute(part, ('tm', 'rows'), [(d, d ^ mask) for d in range(ways)])]
    ppermute x0 -> x7, waiting for transfers between devices: none -> 5.43 us  [on_device(): lax.ppermute(part, ('tm', 'rows'), [(d, d ^ mask) for d in range(ways)])]
  transfers between devices with their start and end apart: 6 -> 13, of which waited for: 2 -> 4; matrix products, arithmetic and copies ran while one was open for 37% -> 39% of each run, Pallas kernels for 0% -> 0%
where the time goes in v1:
time: 94.4 us; the launch traced here: 93.6 us
  local copies, waits for them, and re-layouts  38.5 us (41%)
  starting transfers between devices  20.5 us (22%)
  waiting for transfers between devices  17.5 us (19%)
  matrix products  10.2 us (11%)
  other arithmetic  5.43 us (6%)
  between operations  1.49 us (2%)
    rev x18, local copies, waits for them, and re-layouts, transposed_conv(): kernel_slice = kernel[2 - time_tap, 2 - row_tap, ::-1]  26.5 us
    ppermute x7, starting transfers between devices, on_device(): lax.ppermute(part, ('tm', 'rows'), [(d, d ^ mask) for d in range(ways)])  10.5 us
    ppermute x2, waiting for transfers between devices, shifted(): return lax.ppermute(value, axis, pairs)  10.3 us
    dot_general x18, matrix products, transposed_conv(): jnp.einsum('frwkc,kdc->frwd', stacked, kernel_slice, preferred_element_ty...  10.2 us
    slice x2, local copies, waits for them, and re-layouts, transposed_conv(): kernel_slice = kernel[2 - time_tap, 2 - row_tap, ::-1]  8.09 us
    ppermute x7, waiting for transfers between devices, on_device(): lax.ppermute(part, ('tm', 'rows'), [(d, d ^ mask) for d in range(ways)])  5.43 us
    ppermute x2, starting transfers between devices, with_halo(): lax.ppermute(lax.slice_in_dim(block, block.shape[dim] - width, None, axis...  4.57 us
    ppermute x2, starting transfers between devices, shifted(): return lax.ppermute(value, axis, pairs)  2.89 us
  transfers between devices with their start and end apart: 13, of which 4 were waited for; matrix products, arithmetic and copies ran while one was open for 39% of the time, Pallas kernels for 0%

profile of v1, /device:TPU:0, one launch (start us, length us, event | category | flops | bytes accessed | tf_op | source)
XLA Modules:
  0.0 93.6 jit_solution(8293729342038836590)
XLA Ops:
  1.7 2.4 %collective-permute-start = (bf16[2,1,32,384]{3,2,1,0:T(8,128)(2,1)S(1)}, bf16[2,1,32,384]{3,2,1,0:T(8,128)(2,1)S(1)}, u32[]{:S(2)}, u32[]{:S(2)}) collective-permute-start(bf16[2,1,32,384]{3,2,1,0:T(8,128)(2,1)S(1)} %get-tuple-element.84), channel_id=1, source_target_pairs={{0,1},{2,3},{4,5},{6,7},{8,9},{10,11},{12,13},{14,15},{16,17},{18,... | collective-permute-start | bytes 147464 | tf_op jit(solution)/shard_map/ppermute | solution.py:12
  5.4 5.3 %fusion.104 = (bf16[1,1,3,384,384]{4,3,2,1,0:T(8,128)(2,1)}, bf16[1,1,3,384,384]{4,3,2,1,0:T(8,128)(2,1)S(1)}, bf16[1,1,3,384,384]{4,3,2,1,0:T(8,128)(2,1)S(1)},...) fusion(bf16[3,3,3,384,384]{4,3,2,1,0:T(8,128)(2,1)} %param.10), kind=kLoop, calls=%fused_computation.225 | loop fusion | bytes 15925248 | tf_op jit(solution)/shard_map/slice | solution.py:44
  10.8 2.2 %rev.55 = bf16[1,1,3,384,384]{4,3,2,1,0:T(8,128)(2,1)} reverse(bf16[1,1,3,384,384]{4,3,2,1,0:T(8,128)(2,1)} %get-tuple-element.14), dimensions={2} | reverse | bytes 1769472 | tf_op jit(solution)/shard_map/rev | solution.py:44
  13.0 2.2 %rev.56 = bf16[1,1,3,384,384]{4,3,2,1,0:T(8,128)(2,1)} reverse(bf16[1,1,3,384,384]{4,3,2,1,0:T(8,128)(2,1)} %get-tuple-element.19), dimensions={2} | reverse | bytes 1769472 | tf_op jit(solution)/shard_map/rev | solution.py:44
  15.1 2.2 %rev.57 = bf16[1,1,3,384,384]{4,3,2,1,0:T(8,128)(2,1)} reverse(bf16[1,1,3,384,384]{4,3,2,1,0:T(8,128)(2,1)} %get-tuple-element.18), dimensions={2} | reverse | bytes 1769472 | tf_op jit(solution)/shard_map/rev | solution.py:44
  17.3 2.2 %rev.58 = bf16[1,1,3,384,384]{4,3,2,1,0:T(8,128)(2,1)} reverse(bf16[1,1,3,384,384]{4,3,2,1,0:T(8,128)(2,1)} %get-tuple-element.17), dimensions={2} | reverse | bytes 1769472 | tf_op jit(solution)/shard_map/rev | solution.py:44
  22.0 2.2 %rev.54 = bf16[1,1,3,384,384]{4,3,2,1,0:T(8,128)(2,1)} reverse(bf16[1,1,3,384,384]{4,3,2,1,0:T(8,128)(2,1)} %get-tuple-element.20), dimensions={2} | reverse | bytes 1769472 | tf_op jit(solution)/shard_map/rev | solution.py:44
  24.2 1.4 %collective-permute-start.2 = (bf16[2,6,32,384]{3,2,1,0:T(8,128)(2,1)S(1)}, bf16[2,6,32,384]{3,2,1,0:T(8,128)(2,1)S(1)}, u32[]{:S(2)}, u32[]{:S(2)}) collective-permute-start(bf16[2,6,32,384]{3,2,1,0:T(8,128)(2,1)S(1)} %pad_maximum_fusion.19), channel_id=1, source_target_pairs={{2,0},{4,2},{6,4},{3,1},{5,3},{7,5},{10,8},{12,10},{14,12},{11,9},... | collective-permute-start | bytes 884744 | tf_op jit(solution)/shard_map/ppermute | solution.py:23
  25.8 10.3 %collective-permute-done.2 = bf16[2,6,32,384]{3,2,1,0:T(8,128)(2,1)S(1)} collective-permute-done((bf16[2,6,32,384]{3,2,1,0:T(8,128)(2,1)S(1)}, bf16[2,6,32,384]{3,2,1,0:T(8,128)(2,1)S(1)}, u32[]{:S(2)}, u32[]{:S(2)}) %collective-permute-start.2) | collective-permute-done | bytes 294944 | tf_op jit(solution)/shard_map/ppermute | solution.py:23
  42.4 2.2 %collective-permute-start.3 = (bf16[2,1,32,384]{3,2,1,0:T(8,128)(2,1)S(1)}, bf16[2,1,32,384]{3,2,1,0:T(8,128)(2,1)S(1)}, u32[]{:S(2)}, u32[]{:S(2)}) collective-permute-start(bf16[2,1,32,384]{3,2,1,0:T(8,128)(2,1)S(1)} %get-tuple-element.80), channel_id=1, source_target_pairs={{0,1},{2,3},{4,5},{6,7},{8,9},{10,11},{12,13},{14,15},{16,17},{18,... | collective-permute-start | bytes 147464 | tf_op jit(solution)/shard_map/ppermute | solution.py:12
  45.9 1.8 %collective-permute-done.4 = bf16[2,1,32,384]{3,2,1,0:T(8,128)(2,1)S(1)} collective-permute-done((bf16[2,1,32,384]{3,2,1,0:T(8,128)(2,1)S(1)}, bf16[2,1,32,384]{3,2,1,0:T(8,128)(2,1)S(1)}, u32[]{:S(2)}, u32[]{:S(2)}) %collective-permute-start.4) | collective-permute-done | bytes 49184 | tf_op jit(solution)/shard_map/ppermute | solution.py:15
  48.5 1.5 %collective-permute-start.5 = (bf16[2,6,32,384]{3,2,1,0:T(8,128)(2,1)}, bf16[2,6,32,384]{3,2,1,0:T(8,128)(2,1)}, u32[]{:S(2)}, u32[]{:S(2)}) collective-permute-start(bf16[2,6,32,384]{3,2,1,0:T(8,128)(2,1)} %pad_maximum_fusion.20), channel_id=1, source_target_pairs={{2,0},{4,2},{6,4},{3,1},{5,3},{7,5},{10,8},{12,10},{14,12},{11,9},... | collective-permute-start | bytes 884744 | tf_op jit(solution)/shard_map/ppermute | solution.py:23
  50.0 2.8 %fusion.103 = (bf16[1,1,3,384,384]{4,3,2,1,0:T(8,128)(2,1)}, bf16[1,1,3,384,384]{4,3,2,1,0:T(8,128)(2,1)S(1)}, bf16[1,1,3,384,384]{4,3,2,1,0:T(8,128)(2,1)S(1)},...) fusion(bf16[3,3,3,384,384]{4,3,2,1,0:T(8,128)(2,1)S(1)} %bitcas, ...), kind=kLoop, calls=%fused_computation.224 | loop fusion | bytes 15925248 | tf_op jit(solution)/shard_map/slice | solution.py:44
  52.8 2.2 %rev.63 = bf16[1,1,3,384,384]{4,3,2,1,0:T(8,128)(2,1)} reverse(bf16[1,1,3,384,384]{4,3,2,1,0:T(8,128)(2,1)} %get-tuple-element.5), dimensions={2} | reverse | bytes 1769472 | tf_op jit(solution)/shard_map/rev | solution.py:44
  55.0 2.2 %rev.64 = bf16[1,1,3,384,384]{4,3,2,1,0:T(8,128)(2,1)} reverse(bf16[1,1,3,384,384]{4,3,2,1,0:T(8,128)(2,1)} %get-tuple-element.11), dimensions={2} | reverse | bytes 1769472 | tf_op jit(solution)/shard_map/rev | solution.py:44
  57.2 2.2 %rev.65 = bf16[1,1,3,384,384]{4,3,2,1,0:T(8,128)(2,1)} reverse(bf16[1,1,3,384,384]{4,3,2,1,0:T(8,128)(2,1)} %get-tuple-element.10), dimensions={2} | reverse | bytes 1769472 | tf_op jit(solution)/shard_map/rev | solution.py:44
  59.3 2.2 %rev.66 = bf16[1,1,3,384,384]{4,3,2,1,0:T(8,128)(2,1)} reverse(bf16[1,1,3,384,384]{4,3,2,1,0:T(8,128)(2,1)} %get-tuple-element.9), dimensions={2} | reverse | bytes 1769472 | tf_op jit(solution)/shard_map/rev | solution.py:44
  61.5 2.2 %rev.67 = bf16[1,1,3,384,384]{4,3,2,1,0:T(8,128)(2,1)} reverse(bf16[1,1,3,384,384]{4,3,2,1,0:T(8,128)(2,1)} %get-tuple-element.8), dimensions={2} | reverse | bytes 1769472 | tf_op jit(solution)/shard_map/rev | solution.py:44
  69.1 1.7 %convolution_bitcast_fusion.8 = f32[2,4,32,384]{3,2,0,1:T(8,128)S(1)} fusion(bf16[1,1,3,384,384]{4,3,2,1,0:T(8,128)(2,1)} %rev.63, bf16[2,4,32,1,384]{4,2,1,0,3:T(8,128)(2,1)S(1)} %get-tuple-element.24, bf16[2,4,32,1,384]{4,2,1,0,3:T(8,128)(2,1)S(1)} %get-tuple-element.78, bf16[2,4,32,1,384]{4,2,1,0,3:T(8,128)(2,1)S(1)} %get-tuple-element.23), kind=kOutput, calls=%fused_computation.8 | convolution fusion | flops 227082240 | bytes 1867776 | tf_op jit(solution)/shard_map/frwkc,kdc->frwd/dot_general | solution.py:45
  76.9 2.8 %collective-permute-start.7 = (f32[1,1,2,4,4,384]{5,4,3,2,1,0:T(4,128)S(1)}, f32[1,1,2,4,4,384]{5,4,3,2,1,0:T(4,128)S(1)}, u32[]{:S(2)}, u32[]{:S(2)}) collective-permute-start(f32[1,1,2,4,4,384]{5,4,3,2,1,0:T(4,128)S(1)} %get-tuple-element.70), channel_id=1, source_target_pairs={{0,2},{1,3},{2,0},{3,1},{4,6},{5,7},{6,4},{7,5},{8,10},{9,11},{10,... | collective-permute-start | bytes 147464 | tf_op jit(solution)/shard_map/ppermute | solution.py:86
  79.7 3.5 %collective-permute-start.9 = (f32[1,1,2,4,4,384]{5,4,3,2,1,0:T(4,128)S(1)}, f32[1,1,2,4,4,384]{5,4,3,2,1,0:T(4,128)S(1)}, u32[]{:S(2)}, u32[]{:S(2)}) collective-permute-start(f32[1,1,2,4,4,384]{5,4,3,2,1,0:T(4,128)S(1)} %get-tuple-element.68), channel_id=1, source_target_pairs={{0,4},{1,5},{2,6},{3,7},{4,0},{5,1},{6,2},{7,3},{8,12},{9,13},{10,... | collective-permute-start | bytes 147464 | tf_op jit(solution)/shard_map/ppermute | solution.py:86
  83.2 3.9 %collective-permute-start.11 = (f32[1,1,2,4,4,384]{5,4,3,2,1,0:T(4,128)S(1)}, f32[1,1,2,4,4,384]{5,4,3,2,1,0:T(4,128)S(1)}, u32[]{:S(2)}, u32[]{:S(2)}) collective-permute-start(f32[1,1,2,4,4,384]{5,4,3,2,1,0:T(4,128)S(1)} %get-tuple-element.66), channel_id=1, source_target_pairs={{0,6},{1,7},{2,4},{3,5},{4,2},{5,3},{6,0},{7,1},{8,14},{9,15},{10,... | collective-permute-start | bytes 147464 | tf_op jit(solution)/shard_map/ppermute | solution.py:86
  87.3 3.5 %collective-permute-done.10 = f32[1,1,2,4,4,384]{5,4,3,2,1,0:T(4,128)S(1)} collective-permute-done((f32[1,1,2,4,4,384]{5,4,3,2,1,0:T(4,128)S(1)}, f32[1,1,2,4,4,384]{5,4,3,2,1,0:T(4,128)S(1)}, u32[]{:S(2)}, u32[]{:S(2)}) %collective-permute-start.10) | collective-permute-done | bytes 49184 | tf_op jit(solution)/shard_map/ppermute | solution.py:86
  90.8 2.0 %collective-permute-done.12 = f32[1,1,2,4,4,384]{5,4,3,2,1,0:T(4,128)S(1)} collective-permute-done((f32[1,1,2,4,4,384]{5,4,3,2,1,0:T(4,128)S(1)}, f32[1,1,2,4,4,384]{5,4,3,2,1,0:T(4,128)S(1)}, u32[]{:S(2)}, u32[]{:S(2)}) %collective-permute-start.12) | collective-permute-done | bytes 49184 | tf_op jit(solution)/shard_map/ppermute | solution.py:86
  (118 shorter events, 25.4 us)
Async XLA Ops:
  1.7 22.5 %collective-permute-start = (bf16[2,1,32,384]{3,2,1,0:T(8,128)(2,1)S(1)}, bf16[2,1,32,384]{3,2,1,0:T(8,128)(2,1)S(1)}, u32[]{:S(2)}, u32[]{:S(2)}) collective-permute-start(bf16[2,1,32,384]{3,2,1,0:T(8,128)(2,1)S(1)} %get-tuple-element.84), channel_id=1, source_target_pairs={{0,1},{2,3},{4,5},{6,7},{8,9},{10,11},{12,13},{14,15},{16,17},{18,... | collective-permute-start | bytes 147464 | tf_op jit(solution)/shard_map/ppermute | solution.py:12
  4.1 20.1 %collective-permute-start.1 = (bf16[2,1,32,384]{3,2,1,0:T(8,128)(2,1)S(1)}, bf16[2,1,32,384]{3,2,1,0:T(8,128)(2,1)S(1)}, u32[]{:S(2)}, u32[]{:S(2)}) collective-permute-start(bf16[2,1,32,384]{3,2,1,0:T(8,128)(2,1)S(1)} %get-tuple-element.85), channel_id=1, source_target_pairs={{1,0},{3,2},{5,4},{7,6},{9,8},{11,10},{13,12},{15,14},{17,16},{19,... | collective-permute-start | bytes 147464 | tf_op jit(solution)/shard_map/ppermute | solution.py:15
  10.7 14.9 %copy-start.7 = (bf16[1,2,4,32,384]{4,3,2,1,0:T(8,128)(2,1)S(1)}, bf16[1,2,4,32,384]{4,3,2,1,0:T(8,128)(2,1)}, u32[]{:S(2)}) copy-start(bf16[1,2,4,32,384]{4,3,2,1,0:T(8,128)(2,1)} %param.8) | copy-start | bytes 589828
  24.2 12.9 %copy-start.4 = (bf16[1,1,3,384,384]{4,3,2,1,0:T(8,128)(2,1)S(1)}, bf16[1,1,3,384,384]{4,3,2,1,0:T(8,128)(2,1)}, u32[]{:S(2)}) copy-start(bf16[1,1,3,384,384]{4,3,2,1,0:T(8,128)(2,1)} %rev.55) | copy-start | bytes 2654212
  24.2 13.4 %copy-start.3 = (bf16[1,1,3,384,384]{4,3,2,1,0:T(8,128)(2,1)S(1)}, bf16[1,1,3,384,384]{4,3,2,1,0:T(8,128)(2,1)}, u32[]{:S(2)}) copy-start(bf16[1,1,3,384,384]{4,3,2,1,0:T(8,128)(2,1)} %rev.56) | copy-start | bytes 2654212
  24.2 11.8 %collective-permute-start.2 = (bf16[2,6,32,384]{3,2,1,0:T(8,128)(2,1)S(1)}, bf16[2,6,32,384]{3,2,1,0:T(8,128)(2,1)S(1)}, u32[]{:S(2)}, u32[]{:S(2)}) collective-permute-start(bf16[2,6,32,384]{3,2,1,0:T(8,128)(2,1)S(1)} %pad_maximum_fusion.19), channel_id=1, source_target_pairs={{2,0},{4,2},{6,4},{3,1},{5,3},{7,5},{10,8},{12,10},{14,12},{11,9},... | collective-permute-start | bytes 884744 | tf_op jit(solution)/shard_map/ppermute | solution.py:23
  25.8 12.5 %copy-start.2 = (bf16[1,1,3,384,384]{4,3,2,1,0:T(8,128)(2,1)S(1)}, bf16[1,1,3,384,384]{4,3,2,1,0:T(8,128)(2,1)}, u32[]{:S(2)}) copy-start(bf16[1,1,3,384,384]{4,3,2,1,0:T(8,128)(2,1)} %rev.57) | copy-start | bytes 2654212
  40.0 9.9 %slice-start = ((s8[7962624]{0:T(1024)(128)(4,1)}), s8[4194304]{0:T(1024)(128)(4,1)S(1)}, s32[]{:S(2)}) async-start(s8[7962624]{0:T(1024)(128)(4,1)} %bitcast.326), calls=%async_computation | async-start | bytes 8388608
  41.2 8.8 %slice-start.1 = ((s8[7962624]{0:T(1024)(128)(4,1)}), s8[3768320]{0:T(1024)(128)(4,1)S(1)}, s32[]{:S(2)}) async-start(s8[7962624]{0:T(1024)(128)(4,1)} %bitcast.326), calls=%async_computation.1 | async-start | bytes 7536640
  42.4 6.1 %copy-start.5 = (bf16[2,4,32,384]{3,2,1,0:T(8,128)(2,1)}, bf16[2,4,32,384]{3,2,1,0:T(8,128)(2,1)S(1)}, u32[]{:S(2)}) copy-start(bf16[2,4,32,384]{3,2,1,0:T(8,128)(2,1)S(1)} %fusion.9) | copy-start | bytes 589828
  42.4 3.5 %collective-permute-start.3 = (bf16[2,1,32,384]{3,2,1,0:T(8,128)(2,1)S(1)}, bf16[2,1,32,384]{3,2,1,0:T(8,128)(2,1)S(1)}, u32[]{:S(2)}, u32[]{:S(2)}) collective-permute-start(bf16[2,1,32,384]{3,2,1,0:T(8,128)(2,1)S(1)} %get-tuple-element.80), channel_id=1, source_target_pairs={{0,1},{2,3},{4,5},{6,7},{8,9},{10,11},{12,13},{14,15},{16,17},{18,... | collective-permute-start | bytes 147464 | tf_op jit(solution)/shard_map/ppermute | solution.py:12
  44.6 3.1 %collective-permute-start.4 = (bf16[2,1,32,384]{3,2,1,0:T(8,128)(2,1)S(1)}, bf16[2,1,32,384]{3,2,1,0:T(8,128)(2,1)S(1)}, u32[]{:S(2)}, u32[]{:S(2)}) collective-permute-start(bf16[2,1,32,384]{3,2,1,0:T(8,128)(2,1)S(1)} %get-tuple-element.81), channel_id=1, source_target_pairs={{1,0},{3,2},{5,4},{7,6},{9,8},{11,10},{13,12},{15,14},{17,16},{19,... | collective-permute-start | bytes 147464 | tf_op jit(solution)/shard_map/ppermute | solution.py:15
  48.5 18.7 %collective-permute-start.5 = (bf16[2,6,32,384]{3,2,1,0:T(8,128)(2,1)}, bf16[2,6,32,384]{3,2,1,0:T(8,128)(2,1)}, u32[]{:S(2)}, u32[]{:S(2)}) collective-permute-start(bf16[2,6,32,384]{3,2,1,0:T(8,128)(2,1)} %pad_maximum_fusion.20), channel_id=1, source_target_pairs={{2,0},{4,2},{6,4},{3,1},{5,3},{7,5},{10,8},{12,10},{14,12},{11,9},... | collective-permute-start | bytes 884744 | tf_op jit(solution)/shard_map/ppermute | solution.py:23
  64.7 6.1 %copy-start.6 = (bf16[2,4,32,384]{3,2,1,0:T(8,128)(2,1)S(1)}, bf16[2,4,32,384]{3,2,1,0:T(8,128)(2,1)}, u32[]{:S(2)}) copy-start(bf16[2,4,32,384]{3,2,1,0:T(8,128)(2,1)} %copy-done.5) | copy-start | bytes 589828
  65.9 5.4 %copy-start.14 = (bf16[1,1,3,384,384]{4,3,2,1,0:T(8,128)(2,1)S(1)}, bf16[1,1,3,384,384]{4,3,2,1,0:T(8,128)(2,1)}, u32[]{:S(2)}) copy-start(bf16[1,1,3,384,384]{4,3,2,1,0:T(8,128)(2,1)} %rev.65) | copy-start | bytes 2654212
  66.0 4.8 %copy-start.15 = (bf16[1,1,3,384,384]{4,3,2,1,0:T(8,128)(2,1)S(1)}, bf16[1,1,3,384,384]{4,3,2,1,0:T(8,128)(2,1)}, u32[]{:S(2)}) copy-start(bf16[1,1,3,384,384]{4,3,2,1,0:T(8,128)(2,1)} %rev.64) | copy-start | bytes 2654212
  66.0 5.8 %copy-start.12 = (bf16[1,1,3,384,384]{4,3,2,1,0:T(8,128)(2,1)S(1)}, bf16[1,1,3,384,384]{4,3,2,1,0:T(8,128)(2,1)}, u32[]{:S(2)}) copy-start(bf16[1,1,3,384,384]{4,3,2,1,0:T(8,128)(2,1)} %rev.66) | copy-start | bytes 2654212
  76.6 6.6 %collective-permute-start.6 = (f32[1,1,2,4,4,384]{5,4,3,2,1,0:T(4,128)S(1)}, f32[1,1,2,4,4,384]{5,4,3,2,1,0:T(4,128)S(1)}, u32[]{:S(2)}, u32[]{:S(2)}) collective-permute-start(f32[1,1,2,4,4,384]{5,4,3,2,1,0:T(4,128)S(1)} %get-tuple-element.71), channel_id=1, source_target_pairs={{0,1},{1,0},{2,3},{3,2},{4,5},{5,4},{6,7},{7,6},{8,9},{9,8},{10,11... | collective-permute-start | bytes 147464 | tf_op jit(solution)/shard_map/ppermute | solution.py:86
  76.9 10.2 %collective-permute-start.7 = (f32[1,1,2,4,4,384]{5,4,3,2,1,0:T(4,128)S(1)}, f32[1,1,2,4,4,384]{5,4,3,2,1,0:T(4,128)S(1)}, u32[]{:S(2)}, u32[]{:S(2)}) collective-permute-start(f32[1,1,2,4,4,384]{5,4,3,2,1,0:T(4,128)S(1)} %get-tuple-element.70), channel_id=1, source_target_pairs={{0,2},{1,3},{2,0},{3,1},{4,6},{5,7},{6,4},{7,5},{8,10},{9,11},{10,... | collective-permute-start | bytes 147464 | tf_op jit(solution)/shard_map/ppermute | solution.py:86
  79.7 7.6 %collective-permute-start.8 = (f32[1,1,2,4,4,384]{5,4,3,2,1,0:T(4,128)S(1)}, f32[1,1,2,4,4,384]{5,4,3,2,1,0:T(4,128)S(1)}, u32[]{:S(2)}, u32[]{:S(2)}) collective-permute-start(f32[1,1,2,4,4,384]{5,4,3,2,1,0:T(4,128)S(1)} %get-tuple-element.69), channel_id=1, source_target_pairs={{0,3},{1,2},{2,1},{3,0},{4,7},{5,6},{6,5},{7,4},{8,11},{9,10},{10,... | collective-permute-start | bytes 147464 | tf_op jit(solution)/shard_map/ppermute | solution.py:86
  79.7 7.6 %collective-permute-start.9 = (f32[1,1,2,4,4,384]{5,4,3,2,1,0:T(4,128)S(1)}, f32[1,1,2,4,4,384]{5,4,3,2,1,0:T(4,128)S(1)}, u32[]{:S(2)}, u32[]{:S(2)}) collective-permute-start(f32[1,1,2,4,4,384]{5,4,3,2,1,0:T(4,128)S(1)} %get-tuple-element.68), channel_id=1, source_target_pairs={{0,4},{1,5},{2,6},{3,7},{4,0},{5,1},{6,2},{7,3},{8,12},{9,13},{10,... | collective-permute-start | bytes 147464 | tf_op jit(solution)/shard_map/ppermute | solution.py:86
  83.1 7.7 %collective-permute-start.10 = (f32[1,1,2,4,4,384]{5,4,3,2,1,0:T(4,128)S(1)}, f32[1,1,2,4,4,384]{5,4,3,2,1,0:T(4,128)S(1)}, u32[]{:S(2)}, u32[]{:S(2)}) collective-permute-start(f32[1,1,2,4,4,384]{5,4,3,2,1,0:T(4,128)S(1)} %get-tuple-element.67), channel_id=1, source_target_pairs={{0,5},{1,4},{2,7},{3,6},{4,1},{5,0},{6,3},{7,2},{8,13},{9,12},{10,... | collective-permute-start | bytes 147464 | tf_op jit(solution)/shard_map/ppermute | solution.py:86
  83.2 7.6 %collective-permute-start.11 = (f32[1,1,2,4,4,384]{5,4,3,2,1,0:T(4,128)S(1)}, f32[1,1,2,4,4,384]{5,4,3,2,1,0:T(4,128)S(1)}, u32[]{:S(2)}, u32[]{:S(2)}) collective-permute-start(f32[1,1,2,4,4,384]{5,4,3,2,1,0:T(4,128)S(1)} %get-tuple-element.66), channel_id=1, source_target_pairs={{0,6},{1,7},{2,4},{3,5},{4,2},{5,3},{6,0},{7,1},{8,14},{9,15},{10,... | collective-permute-start | bytes 147464 | tf_op jit(solution)/shard_map/ppermute | solution.py:86
  87.1 5.7 %collective-permute-start.12 = (f32[1,1,2,4,4,384]{5,4,3,2,1,0:T(4,128)S(1)}, f32[1,1,2,4,4,384]{5,4,3,2,1,0:T(4,128)S(1)}, u32[]{:S(2)}, u32[]{:S(2)}) collective-permute-start(f32[1,1,2,4,4,384]{5,4,3,2,1,0:T(4,128)S(1)} %get-tuple-element.65), channel_id=1, source_target_pairs={{0,7},{1,6},{2,5},{3,4},{4,3},{5,2},{6,1},{7,0},{8,15},{9,14},{10,... | collective-permute-start | bytes 147464 | tf_op jit(solution)/shard_map/ppermute | solution.py:86
  (11 other events, 33.6 us)
